TPU v7x, 32 devices: a whole 2x2x4 slice. The times are simulated.
32 devices in a mesh: mode: 16 (over z, y, x), real: 2 (over core).
Axes of the slice: x: 2, y: 2, z: 4, core: 2. Of those that a mesh axis runs over, the one named last changes fastest.
Arguments:
- input_field: bfloat16 [2, 2, 256, 16384], P(None, 'real', 'mode'), may hold values from -6 to 6
- kerr_coeff: bfloat16 [16, 64, 64], P('mode'), may hold values from -0.375 to 0.375
- block_list: int32 [16, 4], P('mode'), may hold values from 0 to 31
Outputs:
- density: float32 [512, 2, 256, 256], P('mode', None, 'real')
All inputs are finite; a program needn't handle non-finite values.
Results may differ from a plain program's by a relative error of at most 0.0085.
Values may be sent and summed in bfloat16 or wider, within the bound.
A program may use at most 64 MiB of HBM per device.

v0:
```python
import math
import jax
import jax.numpy as jnp
from jax import lax
from jax.sharding import PartitionSpec as P

MB = 8
FT = 128
NT = 16384
FB = 32
kerr_strength = 0.25


def kerr_terms(field_blocks, coeff_group, block_group):
    mode_l = jnp.take(field_blocks, block_group[:, 1], axis=2).astype(jnp.float32)
    mode_m = jnp.take(field_blocks, block_group[:, 2], axis=2).astype(jnp.float32)
    mode_n = jnp.take(field_blocks, block_group[:, 3], axis=2).astype(jnp.float32)
    realiz = field_blocks.shape[1]
    group_size = block_group.shape[0]
    steps_local = field_blocks.shape[4]
    prod_re = (
        mode_m[0][:, :, :, None, :] * mode_n[0][:, :, None, :, :]
        + mode_m[1][:, :, :, None, :] * mode_n[1][:, :, None, :, :]
    )
    prod_im = (
        mode_m[1][:, :, :, None, :] * mode_n[0][:, :, None, :, :]
        - mode_m[0][:, :, :, None, :] * mode_n[1][:, :, None, :, :]
    )
    pairs = (
        jnp.stack([prod_re, prod_im])
        .reshape(2, realiz, group_size, MB * MB, steps_local)
        .astype(jnp.bfloat16)
    )
    weighted = jnp.einsum(
        "kab,crkbt->crkat", coeff_group, pairs, preferred_element_type=jnp.float32
    )
    weighted = weighted.reshape(2, realiz, group_size, MB, MB, steps_local)
    term_re = jnp.sum(
        weighted[0] * mode_l[0][:, :, None] - weighted[1] * mode_l[1][:, :, None], axis=3
    )
    term_im = jnp.sum(
        weighted[0] * mode_l[1][:, :, None] + weighted[1] * mode_l[0][:, :, None], axis=3
    )
    one_hot = (
        block_group[:, 0][:, None] == jnp.arange(field_blocks.shape[2], dtype=jnp.int32)[None, :]
    ).astype(jnp.float32)
    return jnp.einsum(
        "kg,crkpt->crgpt", one_hot, jnp.stack([term_re, term_im]), precision=lax.Precision.HIGHEST
    )


def phase_table(extent, modulus):
    index_a = jnp.arange(extent, dtype=jnp.int32)[:, None]
    index_b = jnp.arange(extent, dtype=jnp.int32)[None, :]
    angle = 2.0 * math.pi / modulus * (index_a * index_b % modulus).astype(jnp.float32)
    return (jnp.cos(angle), -jnp.sin(angle))


def first_pass(table, data):
    table_high = table.astype(jnp.bfloat16)
    table_low = (table - table_high.astype(jnp.float32)).astype(jnp.bfloat16)
    upper = jnp.einsum("kn,rmnj->rmkj", table_high, data, preferred_element_type=jnp.float32)
    return upper + jnp.einsum("kn,rmnj->rmkj", table_low, data, preferred_element_type=jnp.float32)


def second_pass(table, data):
    return jnp.einsum("jn,rmkn->rmjk", table, data, precision=lax.Precision.HIGH)


def transform(by_mode):
    realiz = by_mode.shape[1]
    local_modes = by_mode.shape[2]
    signal = by_mode.reshape(2, realiz, local_modes, FT, FT)
    four_re, four_im = phase_table(FT, FT)
    twist_re, twist_im = phase_table(FT, NT)
    half_re = first_pass(four_re, signal[0]) - first_pass(four_im, signal[1])
    half_im = first_pass(four_re, signal[1]) + first_pass(four_im, signal[0])
    turned_re = half_re * twist_re - half_im * twist_im
    turned_im = half_re * twist_im + half_im * twist_re
    out_re = (second_pass(four_re, turned_re) - second_pass(four_im, turned_im)) / FT
    out_im = (second_pass(four_re, turned_im) + second_pass(four_im, turned_re)) / FT
    return jnp.stack([out_re, out_im]).astype(jnp.bfloat16)


def gram_parts(rows_part, cols_part):
    quarters = jnp.einsum(
        "crpbf,drqbf->bcdpq", rows_part, cols_part, preferred_element_type=jnp.float32
    )
    return jnp.stack(
        [quarters[:, 0, 0] + quarters[:, 1, 1], quarters[:, 1, 0] - quarters[:, 0, 1]], axis=1
    )


def shards(input_field, kerr_coeff, block_list):
    timed = lax.all_to_all(input_field, "mode", split_axis=3, concat_axis=2, tiled=True)
    realiz = timed.shape[1]
    width = timed.shape[2]
    steps_local = timed.shape[3]
    field_blocks = timed.reshape(2, realiz, width // MB, MB, steps_local)
    initial = jnp.zeros(field_blocks.shape, jnp.float32)
    running = initial
    coeff_piece = lax.all_gather(kerr_coeff, "mode", axis=0, tiled=True)
    block_piece = lax.all_gather(block_list, "mode", axis=0, tiled=True)
    block_count = block_piece.shape[0]
    coeff_groups = coeff_piece.reshape(
        block_count // 8, 8, coeff_piece.shape[1], coeff_piece.shape[2]
    )
    block_groups = block_piece.reshape(block_count // 8, 8, 4)

    def one_group(carried, groups):
        return (carried + kerr_terms(field_blocks, groups[0], groups[1]), None)

    running, unused = lax.scan(one_group, running, (coeff_groups, block_groups))
    kerr_sum = running
    kerr_sum = kerr_sum.reshape(2, realiz, width, steps_local)
    base = timed.astype(jnp.float32)
    stepped = jnp.stack(
        [base[0] - kerr_strength * kerr_sum[1], base[1] + kerr_strength * kerr_sum[0]]
    ).astype(jnp.bfloat16)
    by_mode = lax.all_to_all(stepped, "mode", split_axis=2, concat_axis=3, tiled=True)
    spectrum = transform(by_mode)
    banded = lax.all_to_all(spectrum, "mode", split_axis=3, concat_axis=2, tiled=True)
    bands_dev = banded.shape[3] * FT // FB
    spec_bands = banded.reshape(2, realiz, width, bands_dev, FB)
    scale = 1.0 / (FB * realiz * lax.axis_size("real"))
    row_count = width // lax.axis_size("real")
    row_first = lax.axis_index("real") * row_count
    shard_piece = lax.all_gather(spec_bands, "real", axis=1, tiled=True)
    own_part = lax.dynamic_slice_in_dim(shard_piece, row_first, row_count, 2)
    return gram_parts(own_part, shard_piece) * scale


def solution(mesh):
    return jax.shard_map(
        shards,
        mesh=mesh,
        in_specs=(P(None, "real", "mode", None), P("mode", None, None), P("mode", None)),
        out_specs=P("mode", None, "real", None),
        check_vma=False,
    )
```

profile of v0, /device:TPU:0, one launch (start us, length us, event | category | flops | bytes accessed | tf_op | source)
XLA Modules:
  0.0 297.2 jit_solution(920240638021889750)
XLA Ops:
  6.5 15.9 %copy.145 = bf16[2,1,16,16384]{2,0,1,3:T(2,128)(2,1)} copy(bf16[2,1,16,16384]{3,2,1,0:T(8,128)(2,1)} %param.7) | data formatting | bytes 2097152 | tf_op args[0]
  22.5 11.2 %reshape.574 = bf16[16,2,16384]{2,1,0:T(2,128)(2,1)} reshape(bf16[16384,1,2,16]{3,2,1,0:T(2,128)(2,1)} %bitcast.267) | data formatting | bytes 2097152
  33.7 8.5 %all-to-all-start = ((bf16[16,2,16384]{2,1,0:T(2,128)(2,1)}), bf16[16,2,16384]{2,1,0:T(2,128)(2,1)S(1)}, u32[]{:S(2)}, u32[]{:S(2)}) async-start(bf16[16,2,16384]{2,1,0:T(2,128)(2,1)} %reshape.574), calls=%async_computation | async-start | bytes 2097152 | tf_op jit(solution)/shard_map/all_to_all | solution.py:95
  42.2 50.9 %all-gather = s32[16,1,4]{2,1,0:T(1,128)S(1)} all-gather(s32[1,1,4]{2,1,0:T(1,128)S(1)} %bitcast.278), channel_id=1, replica_groups=mesh['mode'=16,'real'=2] {'mode'}, dimensions={0}, use_global_device_ids=true | all-gather | bytes 272 | tf_op jit(solution)/shard_map/all_gather | solution.py:103
  93.2 38.7 %all_gather.10 = bf16[16,64,64]{2,1,0:T(8,128)(2,1)S(1)} all-gather(bf16[1,64,64]{2,1,0:T(8,128)(2,1)S(1)} %copy-done.4), channel_id=1, replica_groups=mesh['mode'=16,'real'=2] {'mode'}, dimensions={0}, use_global_device_ids=true | all-gather | bytes 139264 | tf_op jit(solution)/shard_map/all_gather | solution.py:102
  131.8 7.4 %reshape.575 = bf16[16384,1,2,16]{3,2,1,0:T(2,128)(2,1)} reshape(bf16[16,2,16384]{2,1,0:T(2,128)(2,1)S(1)} %all-to-all-done) | data formatting | bytes 2097152
  139.2 17.7 %copy.200 = bf16[2,1,16,16,1024]{4,2,3,0,1:T(8,128)(2,1)S(1)} copy(bf16[2,1,16,16,1024]{2,0,4,3,1:T(2,128)(2,1)} %bitcast.265) | data formatting | bytes 2097152 | tf_op jit(solution)/shard_map/all_to_all | solution.py:95
  156.9 12.7 %copy.197 = bf16[2,1,16,16,1024]{4,3,2,0,1:T(8,128)(2,1)} copy(bf16[2,1,16,16,1024]{2,0,4,3,1:T(2,128)(2,1)} %bitcast.266) | data formatting | bytes 2097152 | tf_op jit(solution)/shard_map/all_to_all | solution.py:95
  169.6 23.4 %while.11 = (s32[]{:T(128)}, f32[2,1,32,8,1024]{4,2,3,0,1:T(8,128)S(1)}, s32[2,8,4]{1,2,0:T(4,128)S(1)}, bf16[2,1,32,8,1024]{4,3,2,1,0:T(8,128)(2,1)S(1)}, bf16[...) while((s32[]{:T(128)}, f32[2,1,32,8,1024]{4,2,3,0,1:T(8,128)S(1)}, ...), condition=%wide.region_3.5_spmd.clone, body=%wide.region_0.4_spmd.clone.sunk | while | flops 198970768 | bytes 36058028 | solution.py:113
  169.7 0.9 copy-done
  170.6 1.8 gather_fusion.2
  172.4 1.8 gather_fusion.1
  174.2 1.8 gather_fusion
  176.4 0.6 fusion.157
  177.0 0.7 convolution_bitcast_fusion.3
  177.7 1.5 subtract_reduce_fusion.2
  179.6 1.7 bitcast_add_fusion.2
  181.4 0.9 copy-done
  182.3 1.8 gather_fusion.2
  184.1 1.8 gather_fusion.1
  185.9 1.8 gather_fusion
  188.1 0.6 fusion.157
  188.8 0.7 convolution_bitcast_fusion.3
  189.5 1.5 subtract_reduce_fusion.2
  191.4 1.7 bitcast_add_fusion.2
  193.1 1.2 copy.152
  194.3 0.2 bitcast_convert_fusion
  194.8 0.6 copy.147
  195.4 0.6 copy.153
  196.1 0.5 fusion.37
  196.7 2.0 copy.155
  198.7 3.7 %all-to-all-start.1 = ((bf16[2,1,256,1024]{3,0,1,2:T(2,128)(2,1)}), bf16[2,1,256,1024]{3,0,1,2:T(2,128)(2,1)S(1)}, u32[]{:S(2)}, u32[]{:S(2)}) async-start(bf16[2,1,256,1024]{3,0,1,2:T(2,128)(2,1)} %copy.155), calls=%async_computation.1 | async-start | bytes 2097152 | tf_op jit(solution)/shard_map/all_to_all | solution.py:120
  202.6 0.3 fusion.78
  203.0 0.3 sine_negate_fusion
  203.3 14.6 %all-to-all-done.1 = bf16[2,1,256,1024]{3,0,1,2:T(2,128)(2,1)S(1)} async-done(((bf16[2,1,256,1024]{3,0,1,2:T(2,128)(2,1)}), bf16[2,1,256,1024]{3,0,1,2:T(2,128)(2,1)S(1)}, u32[]{:S(2)}, u32[]{:S(2)}) %all-to-all-start.1) | async-done | bytes 1048608 | tf_op jit(solution)/shard_map/all_to_all | solution.py:120
  217.9 0.3 copy.156
  218.2 0.9 fusion.137
  219.1 0.3 copy.160
  219.6 0.5 fusion.65
  220.2 0.5 fusion.85
  220.7 1.1 copy.157
  221.8 1.3 reshape.509
  223.1 0.5 fusion.83
  223.6 0.5 fusion.67
  224.2 0.5 convolution_add_fusion.2
  224.7 0.5 convolution_add_fusion.4
  225.3 0.5 fusion.25
  225.8 0.5 fusion.27
  226.4 1.2 fusion.39
  227.6 1.2 fusion.43
  228.8 1.2 fusion.30
  229.9 1.2 fusion.31
  231.2 1.0 copy.173
  232.2 21.6 %all_to_all.45 = bf16[2,1,16,128,128]{4,2,1,0,3:T(8,128)(2,1)S(1)} all-to-all(bf16[2,1,16,128,128]{4,2,1,0,3:T(8,128)(2,1)S(1)} %copy.173), channel_id=1, replica_groups=mesh['mode'=16,'real'=2] {'mode'}, dimensions={3} | all-to-all | bytes 2097152 | tf_op jit(solution)/shard_map/all_to_all | solution.py:122
  253.8 0.4 copy.208
  254.2 0.3 copy.175
  254.5 3.2 %reshape.513 = bf16[2,1,256,32,32]{4,3,2,0,1:T(8,128)(2,1)} reshape(bf16[2,1,16,16,8,128]{5,4,3,2,0,1:T(8,128)(2,1)S(1)} %copy.175) | data formatting | bytes 2097152 | tf_op jit(solution)/shard_map/reshape | solution.py:124
  257.7 5.2 %copy.176 = bf16[2,1,256,32,32]{2,4,1,0,3:T(8,128)(2,1)} copy(bf16[2,1,256,32,32]{4,3,2,0,1:T(8,128)(2,1)} %reshape.513) | data formatting | bytes 2097152 | tf_op jit(solution)/shard_map/reshape | solution.py:124
  263.0 9.0 %all-gather.3.cloned.1.call-done = bf16[2,2,256,32,32]{2,4,1,0,3:T(8,128)(2,1)} async-done(((bf16[2,1,256,32,32]{2,4,1,0,3:T(8,128)(2,1)}), bf16[2,2,256,32,32]{2,4,1,0,3:T(8,128)(2,1)}) %all-gather.3.cloned.1.call-update) | async-done | bytes 2097168 | tf_op jit(solution)/shard_map/all_gather | solution.py:128
  272.0 4.2 %convolution_bitcast_fusion.1 = f32[32,2,2,128,256]{3,4,1,2,0:T(8,128)S(1)} fusion(bf16[2,2,256,32,32]{2,4,1,0,3:T(8,128)(2,1)} %all-gather.3.cloned.1.call-done, s32[]{:T(128)S(6)} %select_n.66), kind=kOutput, calls=%fused_computation.52 | convolution fusion | flops 536870912 | bytes 19922948 | tf_op jit(solution)/shard_map/crpbf,drqbf->bcdpq/dot_general | solution.py:86
  276.2 0.6 fusion.18
  276.9 0.6 fusion.20
  277.5 3.9 %maximum_multiply_fusion = f32[32,2,128,256]{2,3,0,1:T(8,128)} fusion(f32[32,1,128,256]{2,3,0,1:T(8,128)S(1)} %fusion.18, f32[32,1,128,256]{2,3,0,1:T(8,128)S(1)} %fusion.20), kind=kLoop, calls=%fused_computation.53 | loop fusion | flops 4194304 | bytes 16777216 | tf_op jit(solution)/shard_map/mul | solution.py:130
  281.4 8.9 %copy.179 = f32[32,2,128,256]{3,2,1,0:T(8,128)} copy(f32[32,2,128,256]{2,3,0,1:T(8,128)} %maximum_multiply_fusion) | data formatting | bytes 16777216 | tf_op jit(solution)/shard_map/mul | solution.py:130
  (51 shorter events, 2.6 us)
Async XLA Ops:
  33.7 8.5 %copy-start.5 = (s32[1,4]{1,0:T(1,128)S(1)}, s32[1,4]{1,0:T(1,128)}, u32[]{:S(2)}) copy-start(s32[1,4]{1,0:T(1,128)} %param.9) | copy-start | bytes 52
  33.7 59.5 %copy-start.4 = (bf16[1,64,64]{2,1,0:T(8,128)(2,1)S(1)}, bf16[1,64,64]{2,1,0:T(8,128)(2,1)}, u32[]{:S(2)}) copy-start(bf16[1,64,64]{2,1,0:T(8,128)(2,1)} %param.8) | copy-start | bytes 24580
  33.7 98.1 %all-to-all-start = ((bf16[16,2,16384]{2,1,0:T(2,128)(2,1)}), bf16[16,2,16384]{2,1,0:T(2,128)(2,1)S(1)}, u32[]{:S(2)}, u32[]{:S(2)}) async-start(bf16[16,2,16384]{2,1,0:T(2,128)(2,1)} %reshape.574), calls=%async_computation | async-start | bytes 2097152 | tf_op jit(solution)/shard_map/all_to_all | solution.py:95
  169.6 1.0 copy-start
  179.6 1.7 copy-start.1
  181.4 1.0 copy-start
  191.3 1.7 copy-start.1
  193.1 1.2 copy-start.2
  198.7 19.2 %all-to-all-start.1 = ((bf16[2,1,256,1024]{3,0,1,2:T(2,128)(2,1)}), bf16[2,1,256,1024]{3,0,1,2:T(2,128)(2,1)S(1)}, u32[]{:S(2)}, u32[]{:S(2)}) async-start(bf16[2,1,256,1024]{3,0,1,2:T(2,128)(2,1)} %copy.155), calls=%async_computation.1 | async-start | bytes 2097152 | tf_op jit(solution)/shard_map/all_to_all | solution.py:120
  202.4 69.6 %all-gather.3.cloned.1.call-start = ((), (), s32[]{:S(2)}) async-start(), calls=%async_computation.3 | async-start | bytes 3145728 | tf_op jit(solution)/shard_map/all_gather | solution.py:128
  219.6 1.1 copy-start.3
Sparse Core Ops, SparseCore 0:
  263.1 8.8 all-gather.2
where the time goes:
time: 300 us; the launch traced here: 297 us
  blocking collectives  111 us (37%)
  local copies, waits for them, and re-layouts  106 us (35%)
  waiting for transfers between devices  23.6 us (8%)
  matrix products  18.1 us (6%)
  between operations  13.7 us (5%)
  starting transfers between devices  12.3 us (4%)
  other arithmetic  11.5 us (4%)
    all_gather x1, blocking collectives, shards(): block_piece = lax.all_gather(block_list, 'mode', axis=0, tiled=True)  50.9 us
    all_gather x1, blocking collectives, shards(): coeff_piece = lax.all_gather(kerr_coeff, 'mode', axis=0, tiled=True)  38.7 us
    unnamed x12, local copies, waits for them, and re-layouts  34.7 us
    all_to_all x2, local copies, waits for them, and re-layouts, shards(): lax.all_to_all(input_field, 'mode', split_axis=3, concat_axis=2, tiled=True)  30.4 us
    all_to_all x1, blocking collectives, shards(): lax.all_to_all(spectrum, 'mode', split_axis=3, concat_axis=2, tiled=True)  21.6 us
    all_to_all x1, waiting for transfers between devices, shards(): lax.all_to_all(stepped, 'mode', split_axis=2, concat_axis=3, tiled=True)  14.6 us
    all_gather x1, waiting for transfers between devices, shards(): shard_piece = lax.all_gather(spec_bands, 'real', axis=1, tiled=True)  9 us
    mul x1, local copies, waits for them, and re-layouts, shards(): return gram_parts(own_part, shard_piece) * scale  8.94 us
  transfers between devices with their start and end apart: 3, of which 2 were waited for; matrix products, arithmetic and copies ran while one was open for 0% of the time, Pallas kernels for 0%

commit v1 on v0

--- a/solution.py
+++ b/solution.py
@@ -100,7 +100,18 @@
     initial = jnp.zeros(field_blocks.shape, jnp.float32)
     running = initial
     coeff_piece = lax.all_gather(kerr_coeff, "mode", axis=0, tiled=True)
-    block_piece = lax.all_gather(block_list, "mode", axis=0, tiled=True)
+    shaped = lax.axis_index("mode")
+    top = lax.axis_size("mode")
+    current_arr, mixed_arr = (top, shaped)
+    block_piece, back = (block_list, 1)
+    while back < current_arr:
+        b_now = lax.ppermute(
+            block_piece, axis_name="mode", perm=[(i0, i0 ^ back) for i0 in range(current_arr)]
+        )
+        clean = jnp.concatenate([block_piece, b_now], 0)
+        arr_out = jnp.concatenate([b_now, block_piece], 0)
+        block_piece = jnp.where(mixed_arr & back == 0, clean, arr_out)
+        back = 2 * back
     block_count = block_piece.shape[0]
     coeff_groups = coeff_piece.reshape(
         block_count // 8, 8, coeff_piece.shape[1], coeff_piece.shape[2]

time: 300 us -> 275 us (0.917)
  blocking collectives: 111 us -> 72.5 us
  waiting for transfers between devices: 23.6 us -> 34.4 us
    all_gather x1 -> x0, blocking collectives: 50.9 us -> none  [shards(): block_piece = lax.all_gather(block_list, 'mode', axis=0, tiled=True)]
    all_gather x1, blocking collectives: 38.7 us -> 50.7 us  [shards(): coeff_piece = lax.all_gather(kerr_coeff, 'mode', axis=0, tiled=True)]
    ppermute x0 -> x4, waiting for transfers between devices: none -> 10.9 us  [shards(): lax.ppermute(block_piece, axis_name='mode', perm=[(i0, i0 ^ back) for i0...]
  transfers between devices with their start and end apart: 3 -> 7, of which waited for: 2 -> 5; matrix products, arithmetic and copies ran while one was open for 0% -> 0% of each run, Pallas kernels for 0% -> 0%
where the time goes in v1:
time: 275 us; the launch traced here: 271 us
  local copies, waits for them, and re-layouts  104 us (38%)
  blocking collectives  72.5 us (26%)
  waiting for transfers between devices  34.4 us (13%)
  matrix products  19 us (7%)
  starting transfers between devices  15 us (5%)
  between operations  13.7 us (5%)
  other arithmetic  11.8 us (4%)
    all_gather x1, blocking collectives, shards(): coeff_piece = lax.all_gather(kerr_coeff, 'mode', axis=0, tiled=True)  50.7 us
    unnamed x12, local copies, waits for them, and re-layouts  35.3 us
    all_to_all x2, local copies, waits for them, and re-layouts, shards(): lax.all_to_all(input_field, 'mode', split_axis=3, concat_axis=2, tiled=True)  30.4 us
    all_to_all x1, blocking collectives, shards(): lax.all_to_all(spectrum, 'mode', split_axis=3, concat_axis=2, tiled=True)  21.8 us
    all_to_all x1, waiting for transfers between devices, shards(): lax.all_to_all(stepped, 'mode', split_axis=2, concat_axis=3, tiled=True)  14.6 us
    ppermute x4, waiting for transfers between devices, shards(): lax.ppermute(block_piece, axis_name='mode', perm=[(i0, i0 ^ back) for i0...  10.9 us
    all_gather x1, waiting for transfers between devices, shards(): shard_piece = lax.all_gather(spec_bands, 'real', axis=1, tiled=True)  9 us
    mul x1, local copies, waits for them, and re-layouts, shards(): return gram_parts(own_part, shard_piece) * scale  8.94 us
  transfers between devices with their start and end apart: 7, of which 5 were waited for; matrix products, arithmetic and copies ran while one was open for 0% of the time, Pallas kernels for 0%

profile of v1, /device:TPU:0, one launch (start us, length us, event | category | flops | bytes accessed | tf_op | source)
XLA Modules:
  0.0 271.4 jit_solution(5978999099854220259)
XLA Ops:
  6.5 15.9 %copy.151 = bf16[2,1,16,16384]{2,0,1,3:T(2,128)(2,1)} copy(bf16[2,1,16,16384]{3,2,1,0:T(8,128)(2,1)} %param.7) | data formatting | bytes 2097152 | tf_op args[0]
  22.5 11.2 %reshape.572 = bf16[16,2,16384]{2,1,0:T(2,128)(2,1)} reshape(bf16[16384,1,2,16]{3,2,1,0:T(2,128)(2,1)} %bitcast.268) | data formatting | bytes 2097152
  33.7 8.5 %all-to-all-start = ((bf16[16,2,16384]{2,1,0:T(2,128)(2,1)}), bf16[16,2,16384]{2,1,0:T(2,128)(2,1)S(1)}, u32[]{:S(2)}, u32[]{:S(2)}) async-start(bf16[16,2,16384]{2,1,0:T(2,128)(2,1)} %reshape.572), calls=%async_computation | async-start | bytes 2097152 | tf_op jit(solution)/shard_map/all_to_all | solution.py:95
  42.3 1.9 collective-permute-start
  44.2 50.7 %all_gather.6 = bf16[16,64,64]{2,1,0:T(8,128)(2,1)S(1)} all-gather(bf16[1,64,64]{2,1,0:T(8,128)(2,1)S(1)} %copy-done.4), channel_id=1, replica_groups=mesh['mode'=16,'real'=2] {'mode'}, dimensions={0}, use_global_device_ids=true | all-gather | bytes 139264 | tf_op jit(solution)/shard_map/all_gather | solution.py:102
  95.0 3.6 %collective-permute-done.1 = s32[2,4]{0,1:T(4,128)S(1)} collective-permute-done((s32[2,4]{0,1:T(4,128)S(1)}, s32[2,4]{0,1:T(4,128)S(1)}, u32[]{:S(2)}, u32[]{:S(2)}) %collective-permute-start.1) | collective-permute-done | bytes 64 | tf_op jit(solution)/shard_map/ppermute | solution.py:108
  98.6 3.6 %collective-permute-done.2 = s32[4,4]{0,1:T(4,128)S(1)} collective-permute-done((s32[4,4]{0,1:T(4,128)S(1)}, s32[4,4]{0,1:T(4,128)S(1)}, u32[]{:S(2)}, u32[]{:S(2)}) %collective-permute-start.2) | collective-permute-done | bytes 96 | tf_op jit(solution)/shard_map/ppermute | solution.py:108
  102.3 0.7 collective-permute-start.3
  103.0 3.7 %collective-permute-done.3 = s32[8,4]{0,1:T(4,128)S(1)} collective-permute-done((s32[8,4]{0,1:T(4,128)S(1)}, s32[8,4]{0,1:T(4,128)S(1)}, u32[]{:S(2)}, u32[]{:S(2)}) %collective-permute-start.3) | collective-permute-done | bytes 160 | tf_op jit(solution)/shard_map/ppermute | solution.py:108
  106.9 7.4 %reshape.573 = bf16[16384,1,2,16]{3,2,1,0:T(2,128)(2,1)} reshape(bf16[16,2,16384]{2,1,0:T(2,128)(2,1)S(1)} %all-to-all-done) | data formatting | bytes 2097152
  114.3 17.7 %copy.206 = bf16[2,1,16,16,1024]{4,2,3,0,1:T(8,128)(2,1)S(1)} copy(bf16[2,1,16,16,1024]{2,0,4,3,1:T(2,128)(2,1)} %bitcast.266) | data formatting | bytes 2097152 | tf_op jit(solution)/shard_map/all_to_all | solution.py:95
  132.0 12.7 %copy.205 = bf16[2,1,16,16,1024]{4,3,2,0,1:T(8,128)(2,1)} copy(bf16[2,1,16,16,1024]{2,0,4,3,1:T(2,128)(2,1)} %bitcast.267) | data formatting | bytes 2097152 | tf_op jit(solution)/shard_map/all_to_all | solution.py:95
  144.7 23.4 %while.11 = (s32[]{:T(128)}, f32[2,1,32,8,1024]{4,2,3,0,1:T(8,128)S(1)}, s32[2,8,4]{1,0,2:T(2,128)S(1)}, bf16[2,1,32,8,1024]{4,3,2,1,0:T(8,128)(2,1)S(1)}, bf16[...) while((s32[]{:T(128)}, f32[2,1,32,8,1024]{4,2,3,0,1:T(8,128)S(1)}, ...), condition=%wide.region_3.5_spmd.clone, body=%wide.region_0.4_spmd.clone.sunk | while | flops 198970768 | bytes 36058028 | solution.py:124
  144.8 0.9 copy-done
  145.7 1.8 gather_fusion.2
  147.5 1.8 gather_fusion.1
  149.3 1.8 gather_fusion
  151.5 0.6 fusion.157
  152.1 0.7 convolution_bitcast_fusion.3
  152.8 1.5 subtract_reduce_fusion.2
  154.7 1.7 bitcast_add_fusion.2
  156.5 0.9 copy-done
  157.4 1.8 gather_fusion.2
  159.2 1.8 gather_fusion.1
  161.0 1.8 gather_fusion
  163.2 0.6 fusion.157
  163.8 0.7 convolution_bitcast_fusion.3
  164.5 1.5 subtract_reduce_fusion.2
  166.4 1.7 bitcast_add_fusion.2
  168.2 1.2 copy.160
  169.8 0.6 copy.153
  170.4 0.6 copy.161
  171.0 0.5 fusion.37
  171.6 2.0 copy.163
  173.6 3.7 %all-to-all-start.1 = ((bf16[2,1,256,1024]{3,0,1,2:T(2,128)(2,1)}), bf16[2,1,256,1024]{3,0,1,2:T(2,128)(2,1)S(1)}, u32[]{:S(2)}, u32[]{:S(2)}) async-start(bf16[2,1,256,1024]{3,0,1,2:T(2,128)(2,1)} %copy.163), calls=%async_computation.1 | async-start | bytes 2097152 | tf_op jit(solution)/shard_map/all_to_all | solution.py:131
  178.3 14.6 %all-to-all-done.1 = bf16[2,1,256,1024]{3,0,1,2:T(2,128)(2,1)S(1)} async-done(((bf16[2,1,256,1024]{3,0,1,2:T(2,128)(2,1)}), bf16[2,1,256,1024]{3,0,1,2:T(2,128)(2,1)S(1)}, u32[]{:S(2)}, u32[]{:S(2)}) %all-to-all-start.1) | async-done | bytes 1048608 | tf_op jit(solution)/shard_map/all_to_all | solution.py:131
  192.8 0.3 copy.164
  193.2 0.3 copy.168
  193.7 0.5 fusion.65
  194.2 1.5 fusion.85
  195.8 0.3 copy.165
  196.3 0.5 fusion.83
  196.8 0.5 fusion.67
  197.4 0.5 convolution_add_fusion.2
  197.9 0.5 convolution_add_fusion.4
  198.5 0.5 fusion.25
  199.0 0.7 copy-done.3
  199.7 0.5 fusion.27
  200.2 1.2 fusion.39
  201.4 1.2 fusion.43
  202.6 1.2 fusion.30
  203.8 1.2 fusion.31
  205.1 1.0 copy.181
  206.1 21.8 %all_to_all.45 = bf16[2,1,16,128,128]{4,2,1,0,3:T(8,128)(2,1)S(1)} all-to-all(bf16[2,1,16,128,128]{4,2,1,0,3:T(8,128)(2,1)S(1)} %copy.181), channel_id=1, replica_groups=mesh['mode'=16,'real'=2] {'mode'}, dimensions={3} | all-to-all | bytes 2097152 | tf_op jit(solution)/shard_map/all_to_all | solution.py:133
  228.0 0.4 copy.215
  228.4 0.3 copy.183
  228.6 3.2 %reshape.514 = bf16[2,1,256,32,32]{4,3,2,0,1:T(8,128)(2,1)} reshape(bf16[2,1,16,16,8,128]{5,4,3,2,0,1:T(8,128)(2,1)S(1)} %copy.183) | data formatting | bytes 2097152 | tf_op jit(solution)/shard_map/reshape | solution.py:135
  231.9 5.2 %copy.184 = bf16[2,1,256,32,32]{2,4,1,0,3:T(8,128)(2,1)} copy(bf16[2,1,256,32,32]{4,3,2,0,1:T(8,128)(2,1)} %reshape.514) | data formatting | bytes 2097152 | tf_op jit(solution)/shard_map/reshape | solution.py:135
  237.1 9.0 %all-gather.2.cloned.1.call-done = bf16[2,2,256,32,32]{2,4,1,0,3:T(8,128)(2,1)} async-done(((bf16[2,1,256,32,32]{2,4,1,0,3:T(8,128)(2,1)}), bf16[2,2,256,32,32]{2,4,1,0,3:T(8,128)(2,1)}) %all-gather.2.cloned.1.call-update) | async-done | bytes 2097168 | tf_op jit(solution)/shard_map/all_gather | solution.py:139
  246.1 4.2 %convolution_bitcast_fusion.1 = f32[32,2,2,128,256]{3,4,1,2,0:T(8,128)S(1)} fusion(bf16[2,2,256,32,32]{2,4,1,0,3:T(8,128)(2,1)} %all-gather.2.cloned.1.call-done, s32[]{:T(128)S(6)} %select_n.111), kind=kOutput, calls=%fused_computation.52 | convolution fusion | flops 536870912 | bytes 19922948 | tf_op jit(solution)/shard_map/crpbf,drqbf->bcdpq/dot_general | solution.py:86
  250.4 0.6 fusion.18
  251.0 0.6 fusion.20
  251.7 3.9 %maximum_multiply_fusion = f32[32,2,128,256]{2,3,0,1:T(8,128)} fusion(f32[32,1,128,256]{2,3,0,1:T(8,128)S(1)} %fusion.18, f32[32,1,128,256]{2,3,0,1:T(8,128)S(1)} %fusion.20), kind=kLoop, calls=%fused_computation.53 | loop fusion | flops 4194304 | bytes 16777216 | tf_op jit(solution)/shard_map/mul | solution.py:141
  255.6 8.9 %copy.187 = f32[32,2,128,256]{3,2,1,0:T(8,128)} copy(f32[32,2,128,256]{2,3,0,1:T(8,128)} %maximum_multiply_fusion) | data formatting | bytes 16777216 | tf_op jit(solution)/shard_map/mul | solution.py:141
  (63 shorter events, 4.0 us)
Async XLA Ops:
  33.7 8.5 %copy-start.5 = (s32[1,4]{1,0:T(1,128)S(1)}, s32[1,4]{1,0:T(1,128)}, u32[]{:S(2)}) copy-start(s32[1,4]{1,0:T(1,128)} %param.9) | copy-start | bytes 52
  33.7 10.5 %copy-start.4 = (bf16[1,64,64]{2,1,0:T(8,128)(2,1)S(1)}, bf16[1,64,64]{2,1,0:T(8,128)(2,1)}, u32[]{:S(2)}) copy-start(bf16[1,64,64]{2,1,0:T(8,128)(2,1)} %param.8) | copy-start | bytes 24580
  33.7 73.2 %all-to-all-start = ((bf16[16,2,16384]{2,1,0:T(2,128)(2,1)}), bf16[16,2,16384]{2,1,0:T(2,128)(2,1)S(1)}, u32[]{:S(2)}, u32[]{:S(2)}) async-start(bf16[16,2,16384]{2,1,0:T(2,128)(2,1)} %reshape.572), calls=%async_computation | async-start | bytes 2097152 | tf_op jit(solution)/shard_map/all_to_all | solution.py:95
  42.3 52.6 %collective-permute-start = (s32[1,4]{0,1:T(4,128)S(1)}, s32[1,4]{0,1:T(4,128)S(1)}, u32[]{:S(2)}, u32[]{:S(2)}) collective-permute-start(s32[1,4]{0,1:T(4,128)S(1)} %copy.155), channel_id=1, source_target_pairs={{0,2},{2,0},{4,6},{6,4},{8,10},{10,8},{12,14},{14,12},{16,18},{18,... | collective-permute-start | bytes 56 | tf_op jit(solution)/shard_map/ppermute | solution.py:108
  94.9 3.6 %collective-permute-start.1 = (s32[2,4]{0,1:T(4,128)S(1)}, s32[2,4]{0,1:T(4,128)S(1)}, u32[]{:S(2)}, u32[]{:S(2)}) collective-permute-start(s32[2,4]{0,1:T(4,128)S(1)} %add_select_fusion.2), channel_id=1, source_target_pairs={{0,4},{2,6},{4,0},{6,2},{8,12},{10,14},{12,8},{14,10},{16,20},{18,... | collective-permute-start | bytes 104 | tf_op jit(solution)/shard_map/ppermute | solution.py:108
  98.6 3.6 %collective-permute-start.2 = (s32[4,4]{0,1:T(4,128)S(1)}, s32[4,4]{0,1:T(4,128)S(1)}, u32[]{:S(2)}, u32[]{:S(2)}) collective-permute-start(s32[4,4]{0,1:T(4,128)S(1)} %add_select_fusion.3), channel_id=1, source_target_pairs={{0,8},{2,10},{4,12},{6,14},{8,0},{10,2},{12,4},{14,6},{16,24},{18,... | collective-permute-start | bytes 200 | tf_op jit(solution)/shard_map/ppermute | solution.py:108
  102.3 4.5 %collective-permute-start.3 = (s32[8,4]{0,1:T(4,128)S(1)}, s32[8,4]{0,1:T(4,128)S(1)}, u32[]{:S(2)}, u32[]{:S(2)}) collective-permute-start(s32[8,4]{0,1:T(4,128)S(1)} %add_select_fusion.4), channel_id=1, source_target_pairs={{0,16},{2,18},{4,20},{6,22},{8,24},{10,26},{12,28},{14,30},{16,0},... | collective-permute-start | bytes 392 | tf_op jit(solution)/shard_map/ppermute | solution.py:108
  144.7 1.0 copy-start
  154.7 1.7 copy-start.1
  156.4 1.0 copy-start
  166.4 1.7 copy-start.1
  168.1 1.2 copy-start.2
  173.6 19.2 %all-to-all-start.1 = ((bf16[2,1,256,1024]{3,0,1,2:T(2,128)(2,1)}), bf16[2,1,256,1024]{3,0,1,2:T(2,128)(2,1)S(1)}, u32[]{:S(2)}, u32[]{:S(2)}) async-start(bf16[2,1,256,1024]{3,0,1,2:T(2,128)(2,1)} %copy.163), calls=%async_computation.1 | async-start | bytes 2097152 | tf_op jit(solution)/shard_map/all_to_all | solution.py:131
  177.3 68.8 %all-gather.2.cloned.1.call-start = ((), (), s32[]{:S(2)}) async-start(), calls=%async_computation.3 | async-start | bytes 3145728 | tf_op jit(solution)/shard_map/all_gather | solution.py:139
  198.5 1.2 copy-start.3
Sparse Core Ops, SparseCore 0:
  237.2 8.8 all-gather.1
